TPU v7x, 32 devices: a whole 2x2x4 slice. The times are simulated.
32 devices in a mesh: tm: 4 (over x, core), rows: 8 (over z, y).
Axes of the slice: x: 2, y: 2, z: 4, core: 2. Of those that a mesh axis runs over, the one named last changes fastest.
Arguments:
- features: bfloat16 [8, 16, 128, 384], P('tm', 'rows'), may hold values from -6 to 6
- block_gain: float32 [384], replicated, may hold values from 0.5 to 1.5
- conv_weight: bfloat16 [3, 3, 3, 384, 384], replicated, may hold values from -0.0625 to 0.0625
- conv_bias: float32 [384], replicated, may hold values from -3 to 3
- latent_weight: bfloat16 [384, 16], replicated, may hold values from -0.3125 to 0.3125
- latent_bias: float32 [16], replicated, may hold values from -3 to 3
- patch_weight: bfloat16 [64, 5120], replicated, may hold values from -0.75 to 0.75
- patch_bias: float32 [5120], replicated, may hold values from -3 to 3
- shift_mod: float32 [5120], replicated, may hold values from -4 to 4
- scale_mod: float32 [5120], replicated, may hold values from -2 to 2
- query_weight: bfloat16 [5120, 5120], P(None, 'tm'), may hold values from -0.078125 to 0.078125
- query_bias: float32 [5120], P('tm'), may hold values from -4 to 4
- query_gain: float32 [5120], P('tm'), may hold values from 0.5 to 1.5
- key_weight: bfloat16 [5120, 5120], P(None, 'tm'), may hold values from -0.078125 to 0.078125
- key_bias: float32 [5120], P('tm'), may hold values from -4 to 4
- key_gain: float32 [5120], P('tm'), may hold values from 0.5 to 1.5
- packing: int32 [32], replicated, may hold values from 0 to 31, each once
Outputs:
- queries: bfloat16 [4096, 5120], P('rows', 'tm')
- keys: bfloat16 [4096, 5120], P('rows', 'tm')
All inputs are finite; a program needn't handle non-finite values.
Results may differ from a plain program's by a relative error of at most 0.0054.
Values may be sent and summed in bfloat16 or wider, within the bound.
A program may use at most 128 MiB of HBM per device.

v0:
```python
import jax
import jax.numpy as jnp
from jax import lax
from jax.sharding import PartitionSpec as P

epsilon = 1e-06


def with_halo(shard, sides, width):
    for axis, dim in sides:
        size, length = (lax.axis_size(axis), shard.shape[dim])
        up = [(i, (i + 1) % size) for i in range(size - 1)]
        down = [(j, i) for i, j in up]
        last = lax.slice_in_dim(shard, length - width, length, axis=dim)
        leading = lax.slice_in_dim(shard, 0, width, axis=dim)
        before = lax.ppermute(last, axis, up)
        after = lax.ppermute(leading, axis, down)
        shard = jnp.concatenate([before, shard, after], axis=dim)
    return shard


def from_behind(block, axis, distance):
    devices = range(lax.axis_size(axis))
    route = [(i - distance, i) for i in devices if i - distance in devices]
    return lax.ppermute(block, axis, route)


def normed_act(features, block_gain):
    values = features.astype(jnp.float32)
    square_mean = jnp.mean(values * values, axis=-1, keepdims=True)
    return jax.nn.silu(values * lax.rsqrt(square_mean + epsilon) * block_gain).astype(jnp.bfloat16)


def causal_conv(extended, conv_weight, frames, rows_count, cols_count, channels):
    padded = jnp.pad(extended, ((0, 0), (0, 0), (1, 1), (0, 0)))
    total = jnp.zeros((frames * rows_count * cols_count, channels), jnp.float32)
    for depth_at in range(3):
        for row_at in range(3):
            slab_part = padded[depth_at : depth_at + frames, row_at : row_at + rows_count]
            joined = jnp.concatenate(
                [
                    slab_part[:, :, 0:cols_count],
                    slab_part[:, :, 1 : cols_count + 1],
                    slab_part[:, :, 2 : cols_count + 2],
                ],
                axis=-1,
            )
            kernel = conv_weight[depth_at, row_at].reshape(3 * channels, channels)
            total = total + jnp.dot(
                joined.reshape(-1, 3 * channels), kernel, preferred_element_type=jnp.float32
            )
    return total.reshape(frames, rows_count, cols_count, channels)


def per_device(
    features,
    block_gain,
    conv_weight,
    conv_bias,
    latent_weight,
    latent_bias,
    patch_weight,
    patch_bias,
    shift_mod,
    scale_mod,
    query_weight,
    query_bias,
    query_gain,
    key_weight,
    key_bias,
    key_gain,
    packing,
):
    frames, rows_count, cols_count, channels = features.shape
    latent_width = latent_weight.shape[1]
    act = normed_act(features, block_gain)
    rimmed = with_halo(act, (("rows", 1),), 1)
    before = from_behind(rimmed, "tm", 1)
    extended = jnp.concatenate([before, rimmed], axis=0)
    conv = causal_conv(extended, conv_weight, frames, rows_count, cols_count, channels)
    block_out = (features.astype(jnp.float32) + conv + conv_bias).astype(jnp.bfloat16)
    latent = (
        jnp.dot(block_out.reshape(-1, channels), latent_weight, preferred_element_type=jnp.float32)
        + latent_bias
    ).astype(jnp.bfloat16)
    latent = latent.reshape(frames, rows_count // 2, 2, cols_count // 2, 2, latent_width)
    own_block = jnp.transpose(latent, (5, 2, 4, 0, 1, 3)).reshape(4 * latent_width, -1)
    count_tm = lax.axis_size("tm")
    count_rows = lax.axis_size("rows")
    shard = lax.axis_index("rows")
    own_ident = lax.axis_index("tm") * count_rows + shard
    targets = jnp.transpose(packing.reshape(count_rows, count_tm)).reshape(-1)
    marker = (targets == own_ident).astype(jnp.bfloat16)
    outgoing = marker[:, None, None] * own_block[None]
    arrived = lax.all_to_all(outgoing, ("tm", "rows"), split_axis=0, concat_axis=0, tiled=True)
    mine = jnp.sum(arrived.astype(jnp.float32), axis=0).astype(jnp.bfloat16)
    slots = lax.all_gather(mine[None], "tm", axis=0, tiled=True)
    packed = jnp.transpose(slots, (0, 2, 1)).reshape(-1, slots.shape[1])
    embedded = jnp.dot(packed, patch_weight, preferred_element_type=jnp.float32) + patch_bias
    center = jnp.mean(embedded, axis=-1, keepdims=True)
    spread = jnp.mean((embedded - center) ** 2, axis=-1, keepdims=True)
    modulated = (
        (embedded - center) * lax.rsqrt(spread + epsilon) * (1.0 + scale_mod) + shift_mod
    ).astype(jnp.bfloat16)
    query_part = jnp.dot(modulated, query_weight, preferred_element_type=jnp.float32) + query_bias
    key_part = jnp.dot(modulated, key_weight, preferred_element_type=jnp.float32) + key_bias
    width_all = embedded.shape[1]
    query_sum, key_sum = lax.psum(
        (
            jnp.sum(query_part * query_part, axis=-1, keepdims=True),
            jnp.sum(key_part * key_part, axis=-1, keepdims=True),
        ),
        "tm",
    )
    queries = (query_part * lax.rsqrt(query_sum / width_all + epsilon) * query_gain).astype(
        jnp.bfloat16
    )
    keys = (key_part * lax.rsqrt(key_sum / width_all + epsilon) * key_gain).astype(jnp.bfloat16)
    return (queries, keys)


def solution(mesh):
    in_specs = (
        P("tm", "rows", None, None),
        P(),
        P(),
        P(),
        P(),
        P(),
        P(),
        P(),
        P(),
        P(),
        P(None, "tm"),
        P("tm"),
        P("tm"),
        P(None, "tm"),
        P("tm"),
        P("tm"),
        P(),
    )
    out_specs = (P("rows", "tm"), P("rows", "tm"))
    return jax.shard_map(
        per_device, mesh=mesh, in_specs=in_specs, out_specs=out_specs, check_vma=False
    )
```

profile of v0, /device:TPU:0, one launch (start us, length us, event | category | flops | bytes accessed | tf_op | source)
XLA Modules:
  0.0 113.9 jit_solution(17508551514617649937)
XLA Ops:
  0.7 1.2 %fusion.5 = f32[2,2,128]{2,1,0:T(2,128)S(1)} fusion(bf16[2,2,128,384]{3,2,1,0:T(8,128)(2,1)} %param.17), kind=kLoop, calls=%fused_computation.36 | loop fusion | flops 589312 | bytes 395264 | tf_op jit(solution)/shard_map/reduce_sum | solution.py:30
  1.9 1.3 %fusion.12 = bf16[2,2,128,384]{3,2,1,0:T(8,128)(2,1)S(1)} fusion(bf16[2,2,128,384]{3,2,1,0:T(8,128)(2,1)} %param.17, f32[384]{0:T(512)} %param.18, f32[2,2,128]{2,1,0:T(2,128)S(1)} %add_rsqrt_fusion.3), kind=kLoop, calls=%fused_computation.43 | loop fusion | flops 1572864 | bytes 790016 | tf_op jit(solution)/shard_map/convert_element_type | solution.py:31
  3.2 1.3 %collective-permute-start.1 = (bf16[2,1,128,384]{3,2,1,0:T(8,128)(2,1)S(1)}, bf16[2,1,128,384]{3,2,1,0:T(8,128)(2,1)S(1)}, u32[]{:S(2)}, u32[]{:S(2)}) collective-permute-start(bf16[2,1,128,384]{3,2,1,0:T(8,128)(2,1)S(1)} %get-tuple-element.40), channel_id=1, source_target_pairs={{1,0},{2,1},{3,2},{4,3},{5,4},{6,5},{7,6},{9,8},{10,9},{11,10},{12... | collective-permute-start | bytes 589832 | tf_op jit(solution)/shard_map/ppermute | solution.py:17
  4.5 5.5 %collective-permute-start = (bf16[2,1,128,384]{3,2,1,0:T(8,128)(2,1)S(1)}, bf16[2,1,128,384]{3,2,1,0:T(8,128)(2,1)S(1)}, u32[]{:S(2)}, u32[]{:S(2)}) collective-permute-start(bf16[2,1,128,384]{3,2,1,0:T(8,128)(2,1)S(1)} %get-tuple-element.39), channel_id=1, source_target_pairs={{0,1},{1,2},{2,3},{3,4},{4,5},{5,6},{6,7},{8,9},{9,10},{10,11},{11... | collective-permute-start | bytes 589832 | tf_op jit(solution)/shard_map/ppermute | solution.py:16
  10.1 2.9 %collective-permute-done.1 = bf16[2,1,128,384]{3,2,1,0:T(8,128)(2,1)S(1)} collective-permute-done((bf16[2,1,128,384]{3,2,1,0:T(8,128)(2,1)S(1)}, bf16[2,1,128,384]{3,2,1,0:T(8,128)(2,1)S(1)}, u32[]{:S(2)}, u32[]{:S(2)}) %collective-permute-start.1) | collective-permute-done | bytes 196640 | tf_op jit(solution)/shard_map/ppermute | solution.py:17
  13.0 4.4 %collective-permute-done = bf16[2,1,128,384]{3,2,1,0:T(8,128)(2,1)S(1)} collective-permute-done((bf16[2,1,128,384]{3,2,1,0:T(8,128)(2,1)S(1)}, bf16[2,1,128,384]{3,2,1,0:T(8,128)(2,1)S(1)}, u32[]{:S(2)}, u32[]{:S(2)}) %collective-permute-start) | collective-permute-done | bytes 196640 | tf_op jit(solution)/shard_map/ppermute | solution.py:16
  17.4 0.1 pad_maximum_fusion.9
  17.5 2.0 %collective-permute-start.2 = (bf16[2,4,128,384]{3,2,1,0:T(8,128)(2,1)S(1)}, bf16[2,4,128,384]{3,2,1,0:T(8,128)(2,1)S(1)}, u32[]{:S(2)}, u32[]{:S(2)}) collective-permute-start(bf16[2,4,128,384]{3,2,1,0:T(8,128)(2,1)S(1)} %pad_maximum_fusion.9), channel_id=1, source_target_pairs={{0,8},{8,16},{16,24},{1,9},{9,17},{17,25},{2,10},{10,18},{18,26},{... | collective-permute-start | bytes 2359304 | tf_op jit(solution)/shard_map/ppermute | solution.py:25
  19.6 0.1 copy.27
  19.7 0.1 reshape.103
  19.8 3.9 %fusion.18 = (bf16[1,1,3,384,384]{4,3,2,1,0:T(8,128)(2,1)S(1)}, bf16[1,1,3,384,384]{4,3,2,1,0:T(8,128)(2,1)S(1)}, bf16[1,1,3,384,384]{4,3,2,1,0:T(8,128)(2,1)S(1...) fusion(bf16[3,3,3,384,384]{4,3,2,1,0:T(8,128)(2,1)} %param.19), kind=kLoop, calls=%fused_computation.76 | loop fusion | bytes 15925248 | tf_op jit(solution)/shard_map/slice | solution.py:48
  23.8 0.2 maximum_maximum_fusion
  24.0 0.8 pad_slice_fusion.1
  24.8 0.1 pad_slice_fusion.17
  24.9 0.7 pad_slice_fusion
  25.6 0.1 fusion.19
  25.8 0.3 pad_maximum_fusion.2
  26.1 0.8 fusion.21
  26.9 0.8 convolution_add_fusion.9
  27.7 0.3 pad_maximum_fusion.4
  28.0 0.8 convolution_add_fusion.8
  28.8 0.8 convolution_add_fusion.7
  29.6 0.3 pad_maximum_fusion.6
  29.9 0.8 convolution_add_fusion.6
  30.7 0.8 convolution_add_fusion.5
  31.5 0.6 fusion.1
  32.0 0.8 convolution_add_fusion.4
  32.8 0.8 convolution_add_fusion.3
  33.7 0.8 convolution_add_fusion.2
  34.5 0.1 copy-done.3
  34.7 0.1 fusion.14
  34.8 0.2 fusion.4
  35.0 0.1 copy.28
  35.1 0.1 copy.29
  35.2 0.1 mul.107
  35.3 0.9 broadcast_multiply_fusion
  36.2 12.9 %all-to-all-start = ((bf16[32,64,128]{2,1,0:T(8,128)(2,1)}), bf16[32,64,128]{2,1,0:T(8,128)(2,1)S(1)}, u32[]{:S(2)}, u32[]{:S(2)}) async-start(bf16[32,64,128]{2,1,0:T(8,128)(2,1)} %broadcast_multiply_fusion), calls=%async_computation | async-start | bytes 1048576 | tf_op jit(solution)/shard_map/all_to_all | solution.py:95
  49.1 16.2 %all-to-all-done = bf16[32,64,128]{2,1,0:T(8,128)(2,1)S(1)} async-done(((bf16[32,64,128]{2,1,0:T(8,128)(2,1)}), bf16[32,64,128]{2,1,0:T(8,128)(2,1)S(1)}, u32[]{:S(2)}, u32[]{:S(2)}) %all-to-all-start) | async-done | bytes 524320 | tf_op jit(solution)/shard_map/all_to_all | solution.py:95
  65.3 0.1 reduce_sum.58
  65.4 5.4 %all-gather = bf16[256,128]{1,0:T(8,128)(2,1)S(1)} all-gather(bf16[64,128]{1,0:T(8,128)(2,1)S(1)} %reduce_sum.58), channel_id=2, replica_groups=mesh['tm'=4,'rows'=8] {'tm'}, dimensions={0}, use_global_device_ids=true | all-gather | bytes 81920 | tf_op jit(solution)/shard_map/all_gather | solution.py:97
  70.9 1.6 %add_reduce_fusion = (f32[512]{0:T(512)S(1)}, f32[512,5120]{1,0:T(8,128)S(1)}) fusion(f32[5120]{0:T(1024)S(1)} %copy-done.4, bf16[64,5120]{1,0:T(8,128)(2,1)S(1)} %copy-done, bf16[4,8,8,128]{3,2,1,0:T(8,128)(2,1)S(1)} %bitcast.85), kind=kOutput, calls=%fused_computation.2 | convolution fusion | flops 340786688 | bytes 11229184 | tf_op jit(solution)/shard_map/dot_general | solution.py:99
  72.5 1.5 %multiply_reduce_fusion = f32[512]{0:T(512)S(1)} fusion(f32[512,5120]{1,0:T(8,128)S(1)} %get-tuple-element.42, f32[512]{0:T(512)S(1)} %broadcast_multiply_fusion.1, f32[5120]{0:T(1024)S(1)} %copy-done.4), kind=kLoop, calls=%fused_computation.1 | loop fusion | flops 10485248 | bytes 10510336 | tf_op jit(solution)/shard_map/reduce_sum | solution.py:101
  74.0 5.0 %add_convert_fusion = bf16[512,5120]{1,0:T(8,128)(2,1)} fusion(f32[512,5120]{1,0:T(8,128)S(1)} %get-tuple-element.42, f32[5120]{0:T(1024)S(1)} %copy-done.5, f32[5120]{0:T(1024)S(1)} %broadcast_add_fusion, f32[512]{0:T(512)S(1)} %add_rsqrt_fusion.2, f32[512]{0:T(512)S(1)} %broadcast_multiply_fusion.1, f32[5120]{0:T(1024)S(1)} %copy-done.4), kind=kLoop, calls=%fused_computation | loop fusion | flops 15728640 | bytes 15794176 | tf_op jit(solution)/shard_map/convert_element_type | solution.py:104
  79.0 13.9 %multiply_reduce_fusion.2 = (f32[512]{0:T(512)S(1)}, f32[512,1280]{1,0:T(8,128)}) fusion(f32[1280]{0:T(1024)S(1)} %copy-done.12, bf16[512,5120]{1,0:T(8,128)(2,1)} %add_convert_fusion, bf16[5120,1280]{1,0:T(8,128)(2,1)} %param.27), kind=kOutput, calls=%fused_computation.8 | convolution fusion | flops 6712851968 | bytes 20978688 | tf_op jit(solution)/shard_map/dot_general | solution.py:105
  93.0 10.2 %multiply_reduce_fusion.1 = (f32[512]{0:T(512)S(1)}, f32[512,1280]{1,0:T(8,128)S(1)}) fusion(f32[1280]{0:T(1024)S(1)} %copy-done.13, bf16[512,5120]{1,0:T(8,128)(2,1)S(1)} %copy-done.2, bf16[5120,1280]{1,0:T(8,128)(2,1)} %param.30), kind=kOutput, calls=%fused_computation.6 | convolution fusion | flops 6712851968 | bytes 20978688 | tf_op jit(solution)/shard_map/dot_general | solution.py:106
  103.2 6.2 %all-reduce.1 = (f32[512,1]{0,1:T(1,128)S(1)}, f32[512,1]{0,1:T(1,128)S(1)}) all-reduce(f32[512,1]{0,1:T(1,128)S(1)} %bitcast.89, f32[512,1]{0,1:T(1,128)S(1)} %bitcast.90), channel_id=1, replica_groups=mesh['tm'=4,'rows'=8] {'tm'}, use_global_device_ids=true, to_apply=%region_5.6 | all-reduce | flops 1024 | bytes 8192 | tf_op jit(solution)/shard_map/psum | solution.py:108
  109.4 3.1 %multiply_convert_fusion.1 = bf16[512,1280]{1,0:T(8,128)(2,1)} fusion(f32[512,1280]{1,0:T(8,128)} %get-tuple-element.44, f32[1280]{0:T(1024)S(1)} %copy-done.8, f32[512]{0:T(512)S(1)} %bitcast.87), kind=kLoop, calls=%fused_computation.7 | loop fusion | flops 1966080 | bytes 3939328 | tf_op jit(solution)/shard_map/convert_element_type | solution.py:115
  112.5 1.3 %multiply_convert_fusion = bf16[512,1280]{1,0:T(8,128)(2,1)} fusion(f32[512,1280]{1,0:T(8,128)S(1)} %get-tuple-element.46, f32[1280]{0:T(1024)S(1)} %copy-done.9, f32[512]{0:T(512)S(1)} %bitcast.86), kind=kLoop, calls=%fused_computation.5 | loop fusion | flops 1966080 | bytes 3939328 | tf_op jit(solution)/shard_map/convert_element_type | solution.py:118
  (39 shorter events, 0.3 us)
Async XLA Ops:
  0.6 70.2 %copy-start = (bf16[64,5120]{1,0:T(8,128)(2,1)S(1)}, bf16[64,5120]{1,0:T(8,128)(2,1)}, u32[]{:S(2)}) copy-start(bf16[64,5120]{1,0:T(8,128)(2,1)} %param.23) | copy-start | bytes 1966084
  0.6 18.9 %copy-start.14 = (s32[32]{0:T(128)S(1)}, s32[32]{0:T(128)}, u32[]{:S(2)}) copy-start(s32[32]{0:T(128)} %param.33) | copy-start | bytes 388
  3.2 9.8 %collective-permute-start.1 = (bf16[2,1,128,384]{3,2,1,0:T(8,128)(2,1)S(1)}, bf16[2,1,128,384]{3,2,1,0:T(8,128)(2,1)S(1)}, u32[]{:S(2)}, u32[]{:S(2)}) collective-permute-start(bf16[2,1,128,384]{3,2,1,0:T(8,128)(2,1)S(1)} %get-tuple-element.40), channel_id=1, source_target_pairs={{1,0},{2,1},{3,2},{4,3},{5,4},{6,5},{7,6},{9,8},{10,9},{11,10},{12... | collective-permute-start | bytes 589832 | tf_op jit(solution)/shard_map/ppermute | solution.py:17
  4.5 12.9 %collective-permute-start = (bf16[2,1,128,384]{3,2,1,0:T(8,128)(2,1)S(1)}, bf16[2,1,128,384]{3,2,1,0:T(8,128)(2,1)S(1)}, u32[]{:S(2)}, u32[]{:S(2)}) collective-permute-start(bf16[2,1,128,384]{3,2,1,0:T(8,128)(2,1)S(1)} %get-tuple-element.39), channel_id=1, source_target_pairs={{0,1},{1,2},{2,3},{3,4},{4,5},{5,6},{6,7},{8,9},{9,10},{10,11},{11... | collective-permute-start | bytes 589832 | tf_op jit(solution)/shard_map/ppermute | solution.py:16
  17.5 6.2 %collective-permute-start.2 = (bf16[2,4,128,384]{3,2,1,0:T(8,128)(2,1)S(1)}, bf16[2,4,128,384]{3,2,1,0:T(8,128)(2,1)S(1)}, u32[]{:S(2)}, u32[]{:S(2)}) collective-permute-start(bf16[2,4,128,384]{3,2,1,0:T(8,128)(2,1)S(1)} %pad_maximum_fusion.9), channel_id=1, source_target_pairs={{0,8},{8,16},{16,24},{1,9},{9,17},{17,25},{2,10},{10,18},{18,26},{... | collective-permute-start | bytes 2359304 | tf_op jit(solution)/shard_map/ppermute | solution.py:25
  33.6 1.0 copy-start.3
  33.7 1.0 copy-start.10
  33.7 1.1 copy-start.7
  33.7 1.1 copy-start.11
  34.5 14.6 %copy-start.6 = (f32[5120]{0:T(1024)S(1)}, f32[5120]{0:T(1024)}, u32[]{:S(2)}) copy-start(f32[5120]{0:T(1024)} %param.26) | copy-start | bytes 61444
  34.5 36.3 %copy-start.4 = (f32[5120]{0:T(1024)S(1)}, f32[5120]{0:T(1024)}, u32[]{:S(2)}) copy-start(f32[5120]{0:T(1024)} %param.24) | copy-start | bytes 61444
  36.2 29.1 %all-to-all-start = ((bf16[32,64,128]{2,1,0:T(8,128)(2,1)}), bf16[32,64,128]{2,1,0:T(8,128)(2,1)S(1)}, u32[]{:S(2)}, u32[]{:S(2)}) async-start(bf16[32,64,128]{2,1,0:T(8,128)(2,1)} %broadcast_multiply_fusion), calls=%async_computation | async-start | bytes 1048576 | tf_op jit(solution)/shard_map/all_to_all | solution.py:95
  72.5 1.5 %copy-start.5 = (f32[5120]{0:T(1024)S(1)}, f32[5120]{0:T(1024)}, u32[]{:S(2)}) copy-start(f32[5120]{0:T(1024)} %param.25) | copy-start | bytes 61444
  74.0 5.0 %copy-start.12 = (f32[1280]{0:T(1024)S(1)}, f32[1280]{0:T(1024)}, u32[]{:S(2)}) copy-start(f32[1280]{0:T(1024)} %param.28) | copy-start | bytes 15364
  79.0 13.9 %copy-start.2 = (bf16[512,5120]{1,0:T(8,128)(2,1)S(1)}, bf16[512,5120]{1,0:T(8,128)(2,1)}, u32[]{:S(2)}) copy-start(bf16[512,5120]{1,0:T(8,128)(2,1)} %add_convert_fusion) | copy-start | bytes 15728644
  79.0 13.9 %copy-start.13 = (f32[1280]{0:T(1024)S(1)}, f32[1280]{0:T(1024)}, u32[]{:S(2)}) copy-start(f32[1280]{0:T(1024)} %param.31) | copy-start | bytes 15364
  93.0 16.4 %copy-start.8 = (f32[1280]{0:T(1024)S(1)}, f32[1280]{0:T(1024)}, u32[]{:S(2)}) copy-start(f32[1280]{0:T(1024)} %param.29) | copy-start | bytes 15364
  103.2 9.4 %copy-start.9 = (f32[1280]{0:T(1024)S(1)}, f32[1280]{0:T(1024)}, u32[]{:S(2)}) copy-start(f32[1280]{0:T(1024)} %param.32) | copy-start | bytes 15364
  109.4 4.5 %copy-start.1 = (bf16[64,5120]{1,0:T(8,128)(2,1)S(1)}, bf16[64,5120]{1,0:T(8,128)(2,1)}, u32[]{:S(2)}) copy-start(bf16[64,5120]{1,0:T(8,128)(2,1)} %param.23) | copy-start | bytes 1966084
where the time goes:
time: 114 us
  matrix products  33.1 us (29%)
  waiting for transfers between devices  23.5 us (21%)
  starting transfers between devices  21.7 us (19%)
  other arithmetic  16.4 us (14%)
  blocking collectives  11.6 us (10%)
  local copies, waits for them, and re-layouts  6.55 us (6%)
    all_to_all x1, waiting for transfers between devices, per_device(): lax.all_to_all(outgoing, ('tm', 'rows'), split_axis=0, concat_axis=0, til...  16.2 us
    dot_general x1, matrix products, per_device(): jnp.dot(modulated, query_weight, preferred_element_type=jnp.float32)  13.9 us
    all_to_all x1, starting transfers between devices, per_device(): lax.all_to_all(outgoing, ('tm', 'rows'), split_axis=0, concat_axis=0, til...  12.9 us
    dot_general x1, matrix products, per_device(): jnp.dot(modulated, key_weight, preferred_element_type=jnp.float32)  10.2 us
    dot_general x9, matrix products, causal_conv(): jnp.dot(joined.reshape(-1, 3 * channels), kernel, preferred_element_type=...  7.17 us
    psum x1, blocking collectives, per_device(): lax.psum((jnp.sum(query_part * query_part, axis=-1, keepdims=True), jnp.s...  6.16 us
    ppermute x1, starting transfers between devices, with_halo(): before = lax.ppermute(last, axis, up)  5.54 us
    all_gather x1, blocking collectives, per_device(): slots = lax.all_gather(mine[None], 'tm', axis=0, tiled=True)  5.41 us
  transfers between devices with their start and end apart: 4, of which 3 were waited for; matrix products, arithmetic and copies ran while one was open for 4% of the time, Pallas kernels for 0%

commit v1 on v0

v1 whole, which is shorter than its diff:
```python
import functools

import jax
import jax.numpy as jnp
from jax import lax
from jax.experimental import pallas as pl
from jax.experimental.pallas import tpu as pltpu
from jax.sharding import PartitionSpec as P

epsilon = 1e-06
MESH = pl.DeviceIdType.MESH
F32, BF16 = jnp.float32, jnp.bfloat16
HIGH = lax.Precision.HIGHEST


def dot(a, b, **kw):
    return jnp.dot(a, b, preferred_element_type=F32, **kw)


def kernel(
    count_t, count_r,
    packing, feat_h, gain_h, conv_h, cbias_h, lw_h, lbias_h, pw_h, pb_h, shift_h, scale_h,
    wq_h, qb_h, qg_h, wk_h, kb_h, kg_h,
    q_out, k_out,
    feat, gain, conv, cbias, lw, lbias, pw, pb, shift, scale, wq, qb, qg, wk, kb, kg,
    rb, km, lhs, y_ref, fold, snd, rcv, tot, lat_all, emb, mod, qf, kf, sq_q, sq_k, sums_s, sums_r,
    lsem, wsem, hs_sem, hr_sem, as_sem, ar_sem, ss_sem, sr_sem,
):
    t, r = lax.axis_index("tm"), lax.axis_index("rows")
    count = count_t * count_r
    own = t * count_r + r
    _, _, cols, chans = feat.shape
    width = emb.shape[1]
    half = cols // 2
    feats = pw_h.shape[0]
    tokens = mod.shape[0]
    per_block = 2 * half

    small = [(feat_h, feat), (gain_h, gain), (lw_h, lw), (cbias_h, cbias), (lbias_h, lbias)]
    late = [
        (pw_h, pw.at[pl.ds(0, feats)]), (pw_h, pw.at[pl.ds(feats, feats)]), (pb_h, pb), (shift_h, shift),
        (scale_h, scale), (qb_h, qb), (qg_h, qg), (kb_h, kb), (kg_h, kg),
    ]
    copies = [pltpu.make_async_copy(s, d, lsem.at[i]) for i, (s, d) in enumerate(small + late)]
    early, later = copies[: len(small)], copies[len(small) :]
    for c in early:
        c.start()
    conv_copies = [pltpu.make_async_copy(conv_h.at[:, b], conv.at[:, b], wsem.at[b]) for b in range(3)]
    for c in conv_copies:
        c.start()
    for c in later:
        c.start()
    wq_copy = pltpu.make_async_copy(wq_h, wq, wsem.at[3])
    wk_copy = pltpu.make_async_copy(wk_h, wk, wsem.at[4])

    barrier = pltpu.get_barrier_semaphore()

    def greet(i, c):
        other = lax.rem(own + i, count)
        pl.semaphore_signal(barrier, inc=1, device_id=(other // count_r, lax.rem(other, count_r)), device_id_type=MESH)
        return c

    lax.fori_loop(1, count, greet, 0)

    for c in early:
        c.wait()

    lats = lw.shape[1]
    li = lax.broadcasted_iota(jnp.int32, (lats, 2 * feats), 0)
    lj = lax.broadcasted_iota(jnp.int32, (lats, 2 * feats), 1)
    both = ((lj % feats) // 4) == li
    e_both = jnp.where(both, 1.0, 0.0)
    e_low = jnp.where(both & (lj < feats), 1.0, 0.0)
    e_high = jnp.where(both & (lj >= feats), 1.0, 0.0)
    lwv = lw[...]
    lw_low = dot(lwv, e_low.astype(BF16)).astype(BF16)
    lw_high = dot(lwv, e_high.astype(BF16)).astype(BF16)
    lw_both = dot(lwv, e_both.astype(BF16)).astype(BF16)
    span = 2 * feats
    rb[...] = jnp.zeros(rb.shape, BF16)
    rb[pl.ds(0, chans), pl.ds(0, span)] = lw_low
    rb[pl.ds(chans, chans), pl.ds(0, span)] = lw_high
    rb[pl.ds(2 * chans, chans), pl.ds(span, span)] = lw_both
    km[pl.ds(3 * chans, chans), :] = jnp.zeros((chans, km.shape[1]), BF16)
    km[pl.ds(3 * chans, chans), pl.ds(2 * span, span)] = lw_low
    cb8 = jnp.broadcast_to(cbias[...].reshape(1, chans), (8, chans))
    lb8 = jnp.broadcast_to(lbias[...].reshape(1, lats), (8, lats))
    bias8 = dot(cb8, lw_both.astype(F32), precision=HIGH) + dot(lb8, e_both, precision=HIGH)

    gain_v = gain[...].reshape(1, chans)
    row_at = lax.broadcasted_iota(jnp.int32, (cols, chans), 0)
    for f in range(2):
        for w in range(2):
            raw = feat[f, w]
            v = raw.astype(F32)
            sm = jnp.mean(v * v, axis=-1, keepdims=True)
            x = v * lax.rsqrt(sm + epsilon) * gain_v
            act = (x / (1.0 + jnp.exp(-x))).astype(BF16)
            a32 = act.astype(F32)
            prev = jnp.where(row_at == 0, 0.0, pltpu.roll(a32, 1, 0))
            nxt = jnp.where(row_at == cols - 1, 0.0, pltpu.roll(a32, cols - 1, 0))
            at = pl.ds((f * 2 + w) * cols, cols)
            lhs[at, pl.ds(0, chans)] = prev.astype(BF16)
            lhs[at, pl.ds(chans, chans)] = act
            lhs[at, pl.ds(2 * chans, chans)] = nxt.astype(BF16)
            lhs[at, pl.ds(3 * chans, chans)] = raw

    rbv = rb[...]
    for b in range(3):
        conv_copies[b].wait()
        if b == 2:
            wq_copy.start()
            wk_copy.start()
        for e in range(3):
            w3 = jnp.concatenate([conv[2, b, e], conv[1, b, e], conv[0, b, e]], axis=1)
            km[pl.ds(e * chans, chans), pl.ds(b * 2 * span, 2 * span)] = dot(w3, rbv).astype(BF16)

    y_ref[...] = dot(lhs[...], km[...])

    lane = lax.broadcasted_iota(jnp.int32, (cols, span), 1)
    row = lax.broadcasted_iota(jnp.int32, (cols, span), 0)
    even_row = (lane & 2) == 0
    low = lane < feats
    parity = (lane & 1) == (row & 1)

    def y(f, w, b, z):
        return y_ref[pl.ds((f * 2 + w) * cols, cols), pl.ds(b * 2 * span + z * span, span)]

    def mid(f, z):
        return jnp.where(even_row, y(f, 0, 1, z) + y(f, 1, 2, z), y(f, 0, 0, z) + y(f, 1, 1, z))

    def up(f, z):
        return jnp.where(even_row, 0.0, y(f, 0, 2, z))

    def down(f, z):
        return jnp.where(even_row, y(f, 1, 0, z), 0.0)

    for i, part in enumerate((mid, up, down)):
        x0, x1 = part(0, 0), pltpu.roll(part(1, 0), feats, 1)
        mine = jnp.where(low, x0, x0 + x1)
        after = jnp.where(low, x1 + part(0, 1), part(1, 1))
        fold[i] = jnp.where(parity, mine, 0.0)
        fold[3 + i] = jnp.where(parity, after, 0.0)
    for i in range(6):
        snd[i] = fold[i, pl.ds(0, half, 2), :] + fold[i, pl.ds(1, half, 2), :]

    pl.semaphore_wait(barrier, count - 1)

    has_up, has_down = r > 0, r < count_r - 1
    has_next, has_prev = t < count_t - 1, t > 0
    plan = [
        (1, 0, t, r - 1, has_up, has_down),
        (2, 1, t, r + 1, has_down, has_up),
        (3, 2, t + 1, r, has_next, has_prev),
        (4, 3, t + 1, r - 1, has_next & has_up, has_prev & has_down),
        (5, 4, t + 1, r + 1, has_next & has_down, has_prev & has_up),
    ]
    halo = [
        pltpu.make_async_remote_copy(
            src_ref=snd.at[s], dst_ref=rcv.at[d], send_sem=hs_sem.at[d], recv_sem=hr_sem.at[d],
            device_id=(dt, dr), device_id_type=MESH,
        )
        for s, d, dt, dr, _, _ in plan
    ]
    for copy, (_, _, _, _, sends, _) in zip(halo, plan):
        pl.when(sends)(copy.start)
    tot[...] = snd[0] + bias8[0:1, :]
    for copy, (_, d, _, _, _, gets) in zip(halo, plan):
        def take(copy=copy, d=d):
            copy.wait_recv()
            tot[...] += rcv[d]
        pl.when(gets)(take)
    lat_all[own] = tot[...].astype(BF16)

    def to_all(i):
        other = lax.rem(own + i, count)
        return pltpu.make_async_remote_copy(
            src_ref=lat_all.at[own], dst_ref=lat_all.at[own], send_sem=as_sem.at[i], recv_sem=ar_sem.at[own],
            device_id=(other // count_r, lax.rem(other, count_r)), device_id_type=MESH,
        )

    def from_one(i):
        other = lax.rem(own + i, count)
        return pltpu.make_async_remote_copy(
            src_ref=lat_all.at[other], dst_ref=lat_all.at[other], send_sem=as_sem.at[i], recv_sem=ar_sem.at[other],
            device_id=(other // count_r, lax.rem(other, count_r)), device_id_type=MESH,
        )

    def send(i, c):
        to_all(i).start()
        return c

    lax.fori_loop(1, count, send, 0)
    for c in later:
        c.wait()

    def arrive(i, c):
        from_one(i).wait_recv()
        return c

    lax.fori_loop(1, count, arrive, 0)

    step = 512
    plane = lax.broadcasted_iota(jnp.int32, (half, span), 1)

    def lanes_sum(v):
        out = v[:, 0:128]
        for i in range(1, v.shape[1] // 128):
            out = out + v[:, i * 128 : (i + 1) * 128]
        return out

    def block(j, carry):
        p32 = lat_all[packing[r * count_t + j]].astype(F32)
        left = jnp.concatenate(
            [jnp.where(plane < feats, p32, 0.0), jnp.where(plane < feats, 0.0, p32)], axis=0
        ).astype(BF16)
        total = jnp.zeros((per_block, 128), F32)
        for c in range(0, width, step):
            e = dot(left, pw[:, c : c + step]) + pb[pl.ds(c, step)].reshape(1, step)
            emb[:, c : c + step] = e
            total = total + lanes_sum(e)
        center = jnp.sum(total, axis=1, keepdims=True) / width
        total = jnp.zeros((per_block, 128), F32)
        for c in range(0, width, step):
            d = emb[:, c : c + step] - center
            total = total + lanes_sum(d * d)
        inv = lax.rsqrt(jnp.sum(total, axis=1, keepdims=True) / width + epsilon)
        at = pl.ds(pl.multiple_of(j * per_block, per_block), per_block)
        for c in range(0, width, step):
            gains = 1.0 + scale[pl.ds(c, step)].reshape(1, step)
            moved = shift[pl.ds(c, step)].reshape(1, step)
            mod[at, c : c + step] = ((emb[:, c : c + step] - center) * inv * gains + moved).astype(BF16)
        return carry

    lax.fori_loop(0, count_t, block, 0)

    part = qf.shape[1]
    tile = 256 if part % 256 == 0 else 128
    for copy, w, bias, out, sq in ((wq_copy, wq, qb, qf, sq_q), (wk_copy, wk, kb, kf, sq_k)):
        copy.wait()
        sq[...] = jnp.zeros(sq.shape, F32)

        def project(n, carry, w=w, bias=bias, out=out, sq=sq):
            at = pl.ds(pl.multiple_of(n * tile, tile), tile)
            v = dot(mod[...], w[:, at]) + bias[at].reshape(1, tile)
            out[:, at] = v
            sq[...] += lanes_sum(v * v)
            return carry

        lax.fori_loop(0, part // tile, project, 0)

    ones = jnp.ones((4, 128), F32)
    nt = (((1,), (1,)), ((), ()))
    sums_s[...] = jnp.concatenate(
        [
            lax.dot_general(ones, sq_q[...], nt, precision=HIGH, preferred_element_type=F32),
            lax.dot_general(ones, sq_k[...], nt, precision=HIGH, preferred_element_type=F32),
        ],
        axis=0,
    )
    shares = [
        pltpu.make_async_remote_copy(
            src_ref=sums_s, dst_ref=sums_r.at[i - 1], send_sem=ss_sem.at[i - 1], recv_sem=sr_sem.at[i - 1],
            device_id=(lax.rem(t + i, count_t), r), device_id_type=MESH,
        )
        for i in range(1, count_t)
    ]
    for c in shares:
        c.start()
    sums = sums_s[...]
    for i, c in enumerate(shares):
        c.wait_recv()
        sums = sums + sums_r[i]
    inv = lax.rsqrt(sums / width + epsilon)
    pick = lax.broadcasted_iota(jnp.int32, (8, 128), 0)
    tn = (((0,), (0,)), ((), ()))
    inv_q = lax.dot_general(inv, jnp.where(pick == 0, 1.0, 0.0), tn, precision=HIGH, preferred_element_type=F32)
    inv_k = lax.dot_general(inv, jnp.where(pick == 4, 1.0, 0.0), tn, precision=HIGH, preferred_element_type=F32)
    for src, inv_v, gains, out in ((qf, inv_q, qg, q_out), (kf, inv_k, kg, k_out)):
        for c in range(0, part, 128):
            out[:, c : c + 128] = (src[:, c : c + 128] * inv_v * gains[pl.ds(c, 128)].reshape(1, 128)).astype(BF16)

    for copy, (_, _, _, _, sends, _) in zip(halo, plan):
        pl.when(sends)(copy.wait_send)

    def sent(i, c):
        to_all(i).wait_send()
        return c

    lax.fori_loop(1, count, sent, 0)
    for c in shares:
        c.wait_send()


def per_device(
    features, block_gain, conv_weight, conv_bias, latent_weight, latent_bias, patch_weight, patch_bias,
    shift_mod, scale_mod, query_weight, query_bias, query_gain, key_weight, key_bias, key_gain, packing,
):
    count_t, count_r = lax.axis_size("tm"), lax.axis_size("rows")
    count = count_t * count_r
    _, _, cols, chans = features.shape
    feats, width = patch_weight.shape
    part = query_weight.shape[1]
    half = cols // 2
    span = 2 * feats
    tokens = count_t * cols
    V = pltpu.VMEM
    operands = (
        packing, features, block_gain, conv_weight, conv_bias, latent_weight, latent_bias, patch_weight, patch_bias,
        shift_mod, scale_mod, query_weight, query_bias, query_gain, key_weight, key_bias, key_gain,
    )
    like = lambda a: V(a.shape, a.dtype)
    scratch = [like(a) for a in operands[1:7]]
    scratch += [V((2 * feats, width), BF16), like(patch_bias), like(shift_mod), like(scale_mod)]
    scratch += [like(a) for a in operands[11:]]
    scratch += [
        V((3 * chans, 2 * span), BF16),
        V((4 * chans, 6 * span), BF16),
        V((4 * cols, 4 * chans), BF16),
        V((4 * cols, 6 * span), F32),
        V((6, cols, span), F32),
        V((6, half, span), F32),
        V((5, half, span), F32),
        V((half, span), F32),
        V((count, half, span), BF16),
        V((cols, width), F32),
        V((tokens, width), BF16),
        V((tokens, part), F32),
        V((tokens, part), F32),
        V((tokens, 128), F32),
        V((tokens, 128), F32),
        V((8, tokens), F32),
        V((count_t - 1, 8, tokens), F32),
    ]
    dma = pltpu.SemaphoreType.DMA
    scratch += [dma((14,)), dma((5,)), dma((5,)), dma((5,)), dma((count,)), dma((count,)), dma((count_t - 1,)), dma((count_t - 1,))]
    out = jax.ShapeDtypeStruct((tokens, part), BF16)
    return pl.pallas_call(
        functools.partial(kernel, count_t, count_r),
        out_shape=(out, out),
        in_specs=[pl.BlockSpec(memory_space=pltpu.SMEM)] + [pl.BlockSpec(memory_space=pl.ANY)] * 16,
        out_specs=(pl.BlockSpec(memory_space=V),) * 2,
        scratch_shapes=scratch,
        compiler_params=pltpu.CompilerParams(collective_id=0, has_side_effects=True, vmem_limit_bytes=67043328),
    )(*operands)


def solution(mesh):
    in_specs = (
        P("tm", "rows", None, None), P(), P(), P(), P(), P(), P(), P(), P(), P(),
        P(None, "tm"), P("tm"), P("tm"), P(None, "tm"), P("tm"), P("tm"), P(),
    )
    out_specs = (P("rows", "tm"), P("rows", "tm"))
    return jax.shard_map(per_device, mesh=mesh, in_specs=in_specs, out_specs=out_specs, check_vma=False)
```

time: 114 us -> 62.6 us (0.55)
  Pallas kernels: 0 us -> 56.6 us
  matrix products: 33.1 us -> 0 us
  waiting for transfers between devices: 23.5 us -> 0 us
  starting transfers between devices: 21.7 us -> 0 us
  other arithmetic: 16.4 us -> 0 us
  blocking collectives: 11.6 us -> 0 us
  local copies, waits for them, and re-layouts: 6.55 us -> 5.07 us
    pallas_call x0 -> x1, Pallas kernels: none -> 56.6 us  [per_device(): pl.pallas_call(functools.partial(kernel, count_t, count_r), out_shape=(ou...]
    dot_general x13 -> x0, matrix products: 33.1 us -> none  [the longest x1 13.9 us: per_device(): jnp.dot(modulated, query_weight, preferred_element_type=jnp.float32)]
    all_to_all x1 -> x0, waiting for transfers between devices: 16.2 us -> none  [per_device(): lax.all_to_all(outgoing, ('tm', 'rows'), split_axis=0, concat_axis=0, til...]
    all_to_all x1 -> x0, starting transfers between devices: 12.9 us -> none  [per_device(): lax.all_to_all(outgoing, ('tm', 'rows'), split_axis=0, concat_axis=0, til...]
    convert_element_type x6 -> x0, other arithmetic: 10.9 us -> none  [the longest x1 5 us: per_device(): modulated = ((embedded - center) * lax.rsqrt(spread + epsilon) * (1.0 + s...]
    ppermute x3 -> x0, starting transfers between devices: 8.8 us -> none  [the longest x1 5.54 us: with_halo(): before = lax.ppermute(last, axis, up)]
    ppermute x3 -> x0, waiting for transfers between devices: 7.32 us -> none  [the longest x1 4.36 us: with_halo(): before = lax.ppermute(last, axis, up)]
    psum x1 -> x0, blocking collectives: 6.16 us -> none  [per_device(): lax.psum((jnp.sum(query_part * query_part, axis=-1, keepdims=True), jnp.s...]
  transfers between devices with their start and end apart: 4 -> 0, of which waited for: 3 -> 0; matrix products, arithmetic and copies ran while one was open for 4% -> 0% of each run, Pallas kernels for 0% -> 0%
where the time goes in v1:
time: 62.6 us; the launch traced here: 62.4 us
  Pallas kernels  56.6 us (90%)
  local copies, waits for them, and re-layouts  5.07 us (8%)
  between operations  0.65 us (1%)
    pallas_call x1, Pallas kernels, per_device(): pl.pallas_call(functools.partial(kernel, count_t, count_r), out_shape=(ou...  56.6 us
    unnamed x5, local copies, waits for them, and re-layouts  5.07 us

profile of v1, /device:TPU:0, one launch (start us, length us, event | category | flops | bytes accessed | tf_op | source)
XLA Modules:
  0.0 62.4 jit_solution(5945726125743599629)
XLA Ops:
  0.6 1.5 %copy.19.lw_h = bf16[384,16]{1,0:T(8,128)(2,1)} copy(bf16[384,16]{0,1:T(8,128)(2,1)} %param.21) | data formatting | bytes 24576 | tf_op args[4]
  2.1 56.6 %shard_map.176 = (bf16[512,1280]{1,0:T(8,128)(2,1)}, bf16[512,1280]{1,0:T(8,128)(2,1)}) custom-call(s32[32]{0:T(128)} %packing.1, bf16[2,2,128,384]{3,2,1,0:T(8,128)(2,1)} %feat_h.1, f32[384]{0:T(512)} %gain_h.1, bf16[3,3,3,384,384]{4,3,2,1,0:T(8,128)(2,1)} %conv_h.1, f32[384]{0:T(512)} %cbias_h.1, bf16[384,16]{1,0:T(8,128)(2,1)} %copy.19.lw_h, f32[16]{0:T(128)} %lbias_h.1, ...), custom_call_target="tpu_custom_call" | custom-call | tf_op jit(solution)/shard_map/pallas_call | solution.py:338
  58.7 0.0 copy-start
  58.7 2.6 %copy.22 = bf16[512,1280]{1,0:T(8,128)(2,1)} copy(bf16[512,1280]{1,0:T(8,128)(2,1)} %get-tuple-element.4) | data formatting | bytes 2621440
  61.3 0.0 copy-done
  61.3 1.1 %copy.23 = bf16[512,1280]{1,0:T(8,128)(2,1)} copy(bf16[512,1280]{1,0:T(8,128)(2,1)S(1)} %copy-done) | data formatting | bytes 2621440
Async XLA Ops:
  58.7 2.6 %copy-start = (bf16[512,1280]{1,0:T(8,128)(2,1)S(1)}, bf16[512,1280]{1,0:T(8,128)(2,1)}, u32[]{:S(2)}) copy-start(bf16[512,1280]{1,0:T(8,128)(2,1)} %get-tuple-element.5) | copy-start | bytes 3932164

commit v2 on v1

--- a/solution.py
+++ b/solution.py
@@ -20,11 +20,11 @@
 def kernel(
     count_t, count_r,
     packing, feat_h, gain_h, conv_h, cbias_h, lw_h, lbias_h, pw_h, pb_h, shift_h, scale_h,
-    wq_h, qb_h, qg_h, wk_h, kb_h, kg_h,
-    q_out, k_out,
-    feat, gain, conv, cbias, lw, lbias, pw, pb, shift, scale, wq, qb, qg, wk, kb, kg,
-    rb, km, lhs, y_ref, fold, snd, rcv, tot, lat_all, emb, mod, qf, kf, sq_q, sq_k, sums_s, sums_r,
-    lsem, wsem, hs_sem, hr_sem, as_sem, ar_sem, ss_sem, sr_sem,
+    wq_h, qb_h, wk_h, kb_h,
+    q_out, k_out, inv_out,
+    feat, gain, conv, cbias, lw, lbias, pw, pb, shift, scale, wq, qb, wk, kb,
+    rb, km, lhs, y_ref, fold, snd, rcv, tot, lat_all, emb, mod, qf, kf, sq, sums_s, sums_r,
+    lsem, wsem, hs_sem, hr_sem, as_sem, ar_sem, ss_sem, sr_sem, osem,
 ):
     t, r = lax.axis_index("tm"), lax.axis_index("rows")
     count = count_t * count_r
@@ -39,7 +39,7 @@
     small = [(feat_h, feat), (gain_h, gain), (lw_h, lw), (cbias_h, cbias), (lbias_h, lbias)]
     late = [
         (pw_h, pw.at[pl.ds(0, feats)]), (pw_h, pw.at[pl.ds(feats, feats)]), (pb_h, pb), (shift_h, shift),
-        (scale_h, scale), (qb_h, qb), (qg_h, qg), (kb_h, kb), (kg_h, kg),
+        (scale_h, scale), (qb_h, qb), (kb_h, kb),
     ]
     copies = [pltpu.make_async_copy(s, d, lsem.at[i]) for i, (s, d) in enumerate(small + late)]
     early, later = copies[: len(small)], copies[len(small) :]
@@ -65,7 +65,8 @@
     for c in early:
         c.wait()
 
-    lats = lw.shape[1]
+    lats = lw.shape[0]
+    tn = (((0,), (0,)), ((), ()))
     li = lax.broadcasted_iota(jnp.int32, (lats, 2 * feats), 0)
     lj = lax.broadcasted_iota(jnp.int32, (lats, 2 * feats), 1)
     both = ((lj % feats) // 4) == li
@@ -73,9 +74,9 @@
     e_low = jnp.where(both & (lj < feats), 1.0, 0.0)
     e_high = jnp.where(both & (lj >= feats), 1.0, 0.0)
     lwv = lw[...]
-    lw_low = dot(lwv, e_low.astype(BF16)).astype(BF16)
-    lw_high = dot(lwv, e_high.astype(BF16)).astype(BF16)
-    lw_both = dot(lwv, e_both.astype(BF16)).astype(BF16)
+    lw_low = lax.dot_general(lwv, e_low.astype(BF16), tn, preferred_element_type=F32).astype(BF16)
+    lw_high = lax.dot_general(lwv, e_high.astype(BF16), tn, preferred_element_type=F32).astype(BF16)
+    lw_both = lax.dot_general(lwv, e_both.astype(BF16), tn, preferred_element_type=F32).astype(BF16)
     span = 2 * feats
     rb[...] = jnp.zeros(rb.shape, BF16)
     rb[pl.ds(0, chans), pl.ds(0, span)] = lw_low
@@ -172,33 +173,59 @@
         pl.when(gets)(take)
     lat_all[own] = tot[...].astype(BF16)
 
-    def to_all(i):
-        other = lax.rem(own + i, count)
+    side = lax.rem(t, 2)
+    mate = t + 1 - 2 * side
+    group = count // 2
+    place = (t // 2) * count_r + r
+
+    def device(p):
+        return (p // count_r) * 2 + side, lax.rem(p, count_r)
+
+    def spread(i):
+        dt, dr = device(lax.rem(place + i, group))
         return pltpu.make_async_remote_copy(
             src_ref=lat_all.at[own], dst_ref=lat_all.at[own], send_sem=as_sem.at[i], recv_sem=ar_sem.at[own],
-            device_id=(other // count_r, lax.rem(other, count_r)), device_id_type=MESH,
-        )
-
-    def from_one(i):
-        other = lax.rem(own + i, count)
+            device_id=(dt, dr), device_id_type=MESH,
+        )
+
+    def pass_on(i):
+        ft, fr = device(lax.rem(place + group - i, group))
+        ident = ft * count_r + fr
         return pltpu.make_async_remote_copy(
-            src_ref=lat_all.at[other], dst_ref=lat_all.at[other], send_sem=as_sem.at[i], recv_sem=ar_sem.at[other],
-            device_id=(other // count_r, lax.rem(other, count_r)), device_id_type=MESH,
+            src_ref=lat_all.at[ident], dst_ref=lat_all.at[ident], send_sem=as_sem.at[group + i],
+            recv_sem=ar_sem.at[ident], device_id=(mate, r), device_id_type=MESH,
+        )
+
+    def from_mate(i):
+        ft, fr = device(lax.rem(place + group - i, group))
+        ident = (ft + 1 - 2 * side) * count_r + fr
+        return pltpu.make_async_remote_copy(
+            src_ref=lat_all.at[ident], dst_ref=lat_all.at[ident], send_sem=as_sem.at[group + i],
+            recv_sem=ar_sem.at[ident], device_id=(mate, r), device_id_type=MESH,
         )
 
     def send(i, c):
-        to_all(i).start()
-        return c
-
-    lax.fori_loop(1, count, send, 0)
+        spread(i).start()
+        return c
+
+    lax.fori_loop(1, group, send, 0)
+    pass_on(0).start()
     for c in later:
         c.wait()
 
+    def relay(i, c):
+        copy = pass_on(i)
+        copy.wait_recv()
+        copy.start()
+        return c
+
+    lax.fori_loop(1, group, relay, 0)
+
     def arrive(i, c):
-        from_one(i).wait_recv()
-        return c
-
-    lax.fori_loop(1, count, arrive, 0)
+        from_mate(i).wait_recv()
+        return c
+
+    lax.fori_loop(0, group, arrive, 0)
 
     step = 512
     plane = lax.broadcasted_iota(jnp.int32, (half, span), 1)
@@ -236,27 +263,31 @@
 
     part = qf.shape[1]
     tile = 256 if part % 256 == 0 else 128
-    for copy, w, bias, out, sq in ((wq_copy, wq, qb, qf, sq_q), (wk_copy, wk, kb, kf, sq_k)):
+
+    def out_copy(i, n, src, dst):
+        at = pl.ds(pl.multiple_of(n * tile, tile), tile)
+        return pltpu.make_async_copy(src.at[:, at], dst.at[:, at], osem.at[i, n])
+
+    heads = ((wq_copy, wq, qb, qf, q_out), (wk_copy, wk, kb, kf, k_out))
+    for i, (copy, w, bias, src, dst) in enumerate(heads):
         copy.wait()
-        sq[...] = jnp.zeros(sq.shape, F32)
-
-        def project(n, carry, w=w, bias=bias, out=out, sq=sq):
+        lanes = pl.ds(i * 128, 128)
+        sq[:, lanes] = jnp.zeros((tokens, 128), F32)
+
+        def project(n, carry, i=i, w=w, bias=bias, src=src, dst=dst, lanes=lanes):
             at = pl.ds(pl.multiple_of(n * tile, tile), tile)
             v = dot(mod[...], w[:, at]) + bias[at].reshape(1, tile)
-            out[:, at] = v
-            sq[...] += lanes_sum(v * v)
+            src[:, at] = v
+            sq[:, lanes] += lanes_sum(v * v)
+            out_copy(i, n, src, dst).start()
             return carry
 
         lax.fori_loop(0, part // tile, project, 0)
 
-    ones = jnp.ones((4, 128), F32)
+    pick = lax.broadcasted_iota(jnp.int32, (8, 256), 0) // 4 == lax.broadcasted_iota(jnp.int32, (8, 256), 1) // 128
     nt = (((1,), (1,)), ((), ()))
-    sums_s[...] = jnp.concatenate(
-        [
-            lax.dot_general(ones, sq_q[...], nt, precision=HIGH, preferred_element_type=F32),
-            lax.dot_general(ones, sq_k[...], nt, precision=HIGH, preferred_element_type=F32),
-        ],
-        axis=0,
+    sums_s[...] = lax.dot_general(
+        jnp.where(pick, 1.0, 0.0), sq[...], nt, precision=HIGH, preferred_element_type=F32
     )
     shares = [
         pltpu.make_async_remote_copy(
@@ -272,22 +303,28 @@
         c.wait_recv()
         sums = sums + sums_r[i]
     inv = lax.rsqrt(sums / width + epsilon)
-    pick = lax.broadcasted_iota(jnp.int32, (8, 128), 0)
-    tn = (((0,), (0,)), ((), ()))
-    inv_q = lax.dot_general(inv, jnp.where(pick == 0, 1.0, 0.0), tn, precision=HIGH, preferred_element_type=F32)
-    inv_k = lax.dot_general(inv, jnp.where(pick == 4, 1.0, 0.0), tn, precision=HIGH, preferred_element_type=F32)
-    for src, inv_v, gains, out in ((qf, inv_q, qg, q_out), (kf, inv_k, kg, k_out)):
-        for c in range(0, part, 128):
-            out[:, c : c + 128] = (src[:, c : c + 128] * inv_v * gains[pl.ds(c, 128)].reshape(1, 128)).astype(BF16)
+    first = lax.broadcasted_iota(jnp.int32, (8, 128), 0)
+    lane8 = lax.broadcasted_iota(jnp.int32, (8, 128), 1)
+    chosen = jnp.where(first == 4 * (lane8 // 64), 1.0, 0.0)
+    inv_out[...] = lax.dot_general(inv, chosen, tn, precision=HIGH, preferred_element_type=F32)
+    for i, (_, _, _, src, dst) in enumerate(heads):
+        for n in range(part // tile):
+            out_copy(i, n, src, dst).wait()
 
     for copy, (_, _, _, _, sends, _) in zip(halo, plan):
         pl.when(sends)(copy.wait_send)
 
     def sent(i, c):
-        to_all(i).wait_send()
-        return c
-
-    lax.fori_loop(1, count, sent, 0)
+        spread(i).wait_send()
+        return c
+
+    lax.fori_loop(1, group, sent, 0)
+
+    def passed(i, c):
+        pass_on(i).wait_send()
+        return c
+
+    lax.fori_loop(0, group, passed, 0)
     for c in shares:
         c.wait_send()
 
@@ -306,8 +343,8 @@
     tokens = count_t * cols
     V = pltpu.VMEM
     operands = (
-        packing, features, block_gain, conv_weight, conv_bias, latent_weight, latent_bias, patch_weight, patch_bias,
-        shift_mod, scale_mod, query_weight, query_bias, query_gain, key_weight, key_bias, key_gain,
+        packing, features, block_gain, conv_weight, conv_bias, latent_weight.T, latent_bias, patch_weight, patch_bias,
+        shift_mod, scale_mod, query_weight, query_bias, key_weight, key_bias,
     )
     like = lambda a: V(a.shape, a.dtype)
     scratch = [like(a) for a in operands[1:7]]
@@ -327,22 +364,24 @@
         V((tokens, width), BF16),
         V((tokens, part), F32),
         V((tokens, part), F32),
-        V((tokens, 128), F32),
-        V((tokens, 128), F32),
+        V((tokens, 256), F32),
         V((8, tokens), F32),
         V((count_t - 1, 8, tokens), F32),
     ]
     dma = pltpu.SemaphoreType.DMA
-    scratch += [dma((14,)), dma((5,)), dma((5,)), dma((5,)), dma((count,)), dma((count,)), dma((count_t - 1,)), dma((count_t - 1,))]
-    out = jax.ShapeDtypeStruct((tokens, part), BF16)
-    return pl.pallas_call(
+    scratch += [dma((12,)), dma((5,)), dma((5,)), dma((5,)), dma((count,)), dma((count,)), dma((count_t - 1,)), dma((count_t - 1,)), dma((2, part // 128))]
+    out = jax.ShapeDtypeStruct((tokens, part), F32)
+    query, key, inv = pl.pallas_call(
         functools.partial(kernel, count_t, count_r),
-        out_shape=(out, out),
-        in_specs=[pl.BlockSpec(memory_space=pltpu.SMEM)] + [pl.BlockSpec(memory_space=pl.ANY)] * 16,
-        out_specs=(pl.BlockSpec(memory_space=V),) * 2,
+        out_shape=(out, out, jax.ShapeDtypeStruct((tokens, 128), F32)),
+        in_specs=[pl.BlockSpec(memory_space=pltpu.SMEM)] + [pl.BlockSpec(memory_space=pl.ANY)] * 14,
+        out_specs=(pl.BlockSpec(memory_space=pl.ANY),) * 2 + (pl.BlockSpec(memory_space=V),),
         scratch_shapes=scratch,
         compiler_params=pltpu.CompilerParams(collective_id=0, has_side_effects=True, vmem_limit_bytes=67043328),
     )(*operands)
+    queries = (query * inv[:, 0:1] * query_gain).astype(BF16)
+    keys = (key * inv[:, 64:65] * key_gain).astype(BF16)
+    return queries, keys
 
 
 def solution(mesh):

time: 62.6 us -> 57.2 us (0.914)
  Pallas kernels: 56.6 us -> 50.4 us
  other arithmetic: 0 us -> 4.55 us
  local copies, waits for them, and re-layouts: 5.07 us -> 1.38 us
    pallas_call x1, Pallas kernels: 56.6 us -> 50.4 us  [per_device(): pl.pallas_call(functools.partial(kernel, count_t, count_r), out_shape=(ou...]
    unnamed x5 -> x0, local copies, waits for them, and re-layouts: 5.07 us -> none
    convert_element_type x0 -> x1, other arithmetic: none -> 4.55 us  [per_device(): keys = (key * inv[:, 64:65] * key_gain).astype(BF16)]
    slice x0 -> x1, local copies, waits for them, and re-layouts: none -> 1.38 us  [per_device(): keys = (key * inv[:, 64:65] * key_gain).astype(BF16)]
where the time goes in v2:
time: 57.2 us; the launch traced here: 57 us
  Pallas kernels  50.4 us (88%)
  other arithmetic  4.55 us (8%)
  local copies, waits for them, and re-layouts  1.38 us (2%)
  between operations  0.65 us (1%)
    pallas_call x1, Pallas kernels, per_device(): pl.pallas_call(functools.partial(kernel, count_t, count_r), out_shape=(ou...  50.4 us
    convert_element_type x1, other arithmetic, per_device(): keys = (key * inv[:, 64:65] * key_gain).astype(BF16)  4.55 us
    slice x1, local copies, waits for them, and re-layouts, per_device(): keys = (key * inv[:, 64:65] * key_gain).astype(BF16)  1.38 us

profile of v2, /device:TPU:0, one launch (start us, length us, event | category | flops | bytes accessed | tf_op | source)
XLA Modules:
  0.0 57.0 jit_solution(13859903746046379950)
XLA Ops:
  0.6 50.4 %shard_map.176 = (f32[512,1280]{1,0:T(8,128)}, f32[512,1280]{1,0:T(8,128)}, f32[512,128]{1,0:T(8,128)}) custom-call(s32[32]{0:T(128)} %packing.1, bf16[2,2,128,384]{3,2,1,0:T(8,128)(2,1)} %feat_h.1, f32[384]{0:T(512)} %gain_h.1, bf16[3,3,3,384,384]{4,3,2,1,0:T(8,128)(2,1)} %conv_h.1, f32[384]{0:T(512)} %cbias_h.1, bf16[16,384]{1,0:T(8,128)(2,1)} %bitcast.1, ...), custom_call_target="tpu_custom_call" | custom-call | tf_op jit(solution)/shard_map/pallas_call | solution.py:374
  51.1 1.4 %slice_reduce_fusion = (f32[512]{0:T(512)S(1)}, f32[512]{0:T(512)S(1)}) fusion(f32[512,128]{1,0:T(8,128)} %get-tuple-element.6), kind=kLoop, calls=%fused_computation.2 | loop fusion | bytes 8192 | tf_op jit(solution)/shard_map/slice | solution.py:383
  52.4 4.5 %multiply_convert_fusion = (bf16[512,1280]{1,0:T(8,128)(2,1)}, bf16[512,1280]{1,0:T(8,128)(2,1)}) fusion(f32[512,1280]{1,0:T(8,128)} %get-tuple-element.7, f32[1280]{0:T(1024)} %param.32, f32[512]{0:T(512)S(1)} %get-tuple-element.8, f32[1280]{0:T(1024)} %param.29, f32[512,1280]{1,0:T(8,128)} %get-tuple-element.5, f32[512]{0:T(512)S(1)} %get-tuple-element.9), kind=kLoop, calls=%fused_computation | loop fusion | flops 3932160 | bytes 7878656 | tf_op jit(solution)/shard_map/convert_element_type | solution.py:383

commit v3 on v2

--- a/solution.py
+++ b/solution.py
@@ -23,7 +23,7 @@
     wq_h, qb_h, wk_h, kb_h,
     q_out, k_out, inv_out,
     feat, gain, conv, cbias, lw, lbias, pw, pb, shift, scale, wq, qb, wk, kb,
-    rb, km, lhs, y_ref, fold, snd, rcv, tot, lat_all, emb, mod, qf, kf, sq, sums_s, sums_r,
+    rb, km, lhs, y_ref, fold, snd, rcv, tot, lat_all, emb, mod, tiles, sq, sums_s, sums_r,
     lsem, wsem, hs_sem, hr_sem, as_sem, ar_sem, ss_sem, sr_sem, osem,
 ):
     t, r = lax.axis_index("tm"), lax.axis_index("rows")
@@ -115,8 +115,8 @@
         for e in range(3):
             w3 = jnp.concatenate([conv[2, b, e], conv[1, b, e], conv[0, b, e]], axis=1)
             km[pl.ds(e * chans, chans), pl.ds(b * 2 * span, 2 * span)] = dot(w3, rbv).astype(BF16)
-
-    y_ref[...] = dot(lhs[...], km[...])
+        at = pl.ds(b * 2 * span, 2 * span)
+        y_ref[:, at] = dot(lhs[...], km[:, at])
 
     lane = lax.broadcasted_iota(jnp.int32, (cols, span), 1)
     row = lax.broadcasted_iota(jnp.int32, (cols, span), 0)
@@ -261,28 +261,32 @@
 
     lax.fori_loop(0, count_t, block, 0)
 
-    part = qf.shape[1]
-    tile = 256 if part % 256 == 0 else 128
-
-    def out_copy(i, n, src, dst):
+    part = wq.shape[1]
+    tile = tiles.shape[2]
+    count_n = part // tile
+
+    def out_copy(i, n, dst):
         at = pl.ds(pl.multiple_of(n * tile, tile), tile)
-        return pltpu.make_async_copy(src.at[:, at], dst.at[:, at], osem.at[i, n])
-
-    heads = ((wq_copy, wq, qb, qf, q_out), (wk_copy, wk, kb, kf, k_out))
-    for i, (copy, w, bias, src, dst) in enumerate(heads):
+        return pltpu.make_async_copy(tiles.at[lax.rem(i * count_n + n, 2)], dst.at[:, at], osem.at[i, n])
+
+    heads = ((wq_copy, wq, qb, q_out), (wk_copy, wk, kb, k_out))
+    for i, (copy, w, bias, dst) in enumerate(heads):
         copy.wait()
         lanes = pl.ds(i * 128, 128)
         sq[:, lanes] = jnp.zeros((tokens, 128), F32)
 
-        def project(n, carry, i=i, w=w, bias=bias, src=src, dst=dst, lanes=lanes):
+        def project(n, carry, i=i, w=w, bias=bias, dst=dst, lanes=lanes):
             at = pl.ds(pl.multiple_of(n * tile, tile), tile)
+            pl.when(n >= 2)(lambda: out_copy(i, n - 2, dst).wait())
+            if i:
+                pl.when(n < 2)(lambda: out_copy(0, count_n - 2 + n, heads[0][3]).wait())
             v = dot(mod[...], w[:, at]) + bias[at].reshape(1, tile)
-            src[:, at] = v
+            tiles[lax.rem(i * count_n + n, 2)] = v
             sq[:, lanes] += lanes_sum(v * v)
-            out_copy(i, n, src, dst).start()
+            out_copy(i, n, dst).start()
             return carry
 
-        lax.fori_loop(0, part // tile, project, 0)
+        lax.fori_loop(0, count_n, project, 0)
 
     pick = lax.broadcasted_iota(jnp.int32, (8, 256), 0) // 4 == lax.broadcasted_iota(jnp.int32, (8, 256), 1) // 128
     nt = (((1,), (1,)), ((), ()))
@@ -303,13 +307,12 @@
         c.wait_recv()
         sums = sums + sums_r[i]
     inv = lax.rsqrt(sums / width + epsilon)
-    first = lax.broadcasted_iota(jnp.int32, (8, 128), 0)
-    lane8 = lax.broadcasted_iota(jnp.int32, (8, 128), 1)
-    chosen = jnp.where(first == 4 * (lane8 // 64), 1.0, 0.0)
+    first = lax.broadcasted_iota(jnp.int32, (8, 256), 0)
+    lane8 = lax.broadcasted_iota(jnp.int32, (8, 256), 1)
+    chosen = jnp.where(first == 4 * (lane8 // 128), 1.0, 0.0)
     inv_out[...] = lax.dot_general(inv, chosen, tn, precision=HIGH, preferred_element_type=F32)
-    for i, (_, _, _, src, dst) in enumerate(heads):
-        for n in range(part // tile):
-            out_copy(i, n, src, dst).wait()
+    for n in range(count_n - 2, count_n):
+        out_copy(1, n, k_out).wait()
 
     for copy, (_, _, _, _, sends, _) in zip(halo, plan):
         pl.when(sends)(copy.wait_send)
@@ -341,6 +344,7 @@
     half = cols // 2
     span = 2 * feats
     tokens = count_t * cols
+    tile = 256 if part % 256 == 0 else 128
     V = pltpu.VMEM
     operands = (
         packing, features, block_gain, conv_weight, conv_bias, latent_weight.T, latent_bias, patch_weight, patch_bias,
@@ -362,8 +366,7 @@
         V((count, half, span), BF16),
         V((cols, width), F32),
         V((tokens, width), BF16),
-        V((tokens, part), F32),
-        V((tokens, part), F32),
+        V((2, tokens, tile), F32),
         V((tokens, 256), F32),
         V((8, tokens), F32),
         V((count_t - 1, 8, tokens), F32),
@@ -373,15 +376,55 @@
     out = jax.ShapeDtypeStruct((tokens, part), F32)
     query, key, inv = pl.pallas_call(
         functools.partial(kernel, count_t, count_r),
-        out_shape=(out, out, jax.ShapeDtypeStruct((tokens, 128), F32)),
+        out_shape=(out, out, jax.ShapeDtypeStruct((tokens, 256), F32)),
         in_specs=[pl.BlockSpec(memory_space=pltpu.SMEM)] + [pl.BlockSpec(memory_space=pl.ANY)] * 14,
         out_specs=(pl.BlockSpec(memory_space=pl.ANY),) * 2 + (pl.BlockSpec(memory_space=V),),
         scratch_shapes=scratch,
         compiler_params=pltpu.CompilerParams(collective_id=0, has_side_effects=True, vmem_limit_bytes=67043328),
     )(*operands)
-    queries = (query * inv[:, 0:1] * query_gain).astype(BF16)
-    keys = (key * inv[:, 64:65] * key_gain).astype(BF16)
-    return queries, keys
+    return finish(query, key, inv, query_gain, key_gain)
+
+
+def scaled(q_h, k_h, inv, qg, kg, qo_h, ko_h, q, k, qo, ko, in_sem, out_sem):
+    chunks, _, part = q.shape[0], q.shape[1], q.shape[2]
+    rows = q.shape[1]
+    both = ((q_h, q, qg, qo, qo_h), (k_h, k, kg, ko, ko_h))
+    loads, stores = [], []
+    for c in range(chunks):
+        for i, (src, buf, _, obuf, dst) in enumerate(both):
+            at = pl.ds(c * rows, rows)
+            loads.append(pltpu.make_async_copy(src.at[at], buf.at[c], in_sem.at[i, c]))
+            stores.append(pltpu.make_async_copy(obuf.at[c], dst.at[at], out_sem.at[i, c]))
+    for copy in loads:
+        copy.start()
+    for c in range(chunks):
+        for i, (_, buf, gain, obuf, _) in enumerate(both):
+            loads[2 * c + i].wait()
+            factor = inv[pl.ds(c * rows, rows), pl.ds(i * 128, 128)]
+            for n in range(0, part, 128):
+                at = pl.ds(n, 128)
+                obuf[c, :, at] = (buf[c, :, at] * factor * gain[at].reshape(1, 128)).astype(BF16)
+            stores[2 * c + i].start()
+    for copy in stores:
+        copy.wait()
+
+
+def finish(query, key, inv, query_gain, key_gain):
+    tokens, part = query.shape
+    chunks = tokens // 128
+    out = jax.ShapeDtypeStruct((tokens, part), BF16)
+    V, dma = pltpu.VMEM, pltpu.SemaphoreType.DMA
+    return pl.pallas_call(
+        scaled,
+        out_shape=(out, out),
+        in_specs=[pl.BlockSpec(memory_space=pl.ANY)] * 2 + [pl.BlockSpec(memory_space=V)] * 3,
+        out_specs=(pl.BlockSpec(memory_space=pl.ANY),) * 2,
+        scratch_shapes=[
+            V((chunks, 128, part), F32), V((chunks, 128, part), F32), V((chunks, 128, part), BF16), V((chunks, 128, part), BF16),
+            dma((2, chunks)), dma((2, chunks)),
+        ],
+        compiler_params=pltpu.CompilerParams(vmem_limit_bytes=67043328),
+    )(query, key, inv, query_gain, key_gain)
 
 
 def solution(mesh):

time: 57.2 us -> 56.7 us (level)
  Pallas kernels: 50.4 us -> 55.9 us
  other arithmetic: 4.55 us -> 0 us
  local copies, waits for them, and re-layouts: 1.38 us -> 0 us
    pallas_call x0 -> x1, Pallas kernels: none -> 5.05 us  [finish(): pl.pallas_call(scaled, out_shape=(out, out), in_specs=[pl.BlockSpec(memor...]
    convert_element_type x1 -> x0, other arithmetic: 4.55 us -> none  [per_device(): keys = (key * inv[:, 64:65] * key_gain).astype(BF16)]
    slice x1 -> x0, local copies, waits for them, and re-layouts: 1.38 us -> none  [per_device(): keys = (key * inv[:, 64:65] * key_gain).astype(BF16)]
where the time goes in v3:
time: 56.7 us; the launch traced here: 56.5 us
  Pallas kernels  55.9 us (99%)
  between operations  0.64 us (1%)
    pallas_call x1, Pallas kernels, per_device(): pl.pallas_call(functools.partial(kernel, count_t, count_r), out_shape=(ou...  50.8 us
    pallas_call x1, Pallas kernels, finish(): pl.pallas_call(scaled, out_shape=(out, out), in_specs=[pl.BlockSpec(memor...  5.05 us

profile of v3, /device:TPU:0, one launch (start us, length us, event | category | flops | bytes accessed | tf_op | source)
XLA Modules:
  0.0 56.5 jit_solution(5336177378088129129)
XLA Ops:
  0.6 50.8 %shard_map.176 = (f32[512,1280]{1,0:T(8,128)}, f32[512,1280]{1,0:T(8,128)}, f32[512,256]{1,0:T(8,128)}) custom-call(s32[32]{0:T(128)} %packing.1, bf16[2,2,128,384]{3,2,1,0:T(8,128)(2,1)} %feat_h.1, f32[384]{0:T(512)} %gain_h.1, bf16[3,3,3,384,384]{4,3,2,1,0:T(8,128)(2,1)} %conv_h.1, f32[384]{0:T(512)} %cbias_h.1, bf16[16,384]{1,0:T(8,128)(2,1)} %bitcast.1, ...), custom_call_target="tpu_custom_call" | custom-call | tf_op jit(solution)/shard_map/pallas_call | solution.py:377
  51.5 5.1 %shard_map.177 = (bf16[512,1280]{1,0:T(8,128)(2,1)}, bf16[512,1280]{1,0:T(8,128)(2,1)}) custom-call(f32[512,1280]{1,0:T(8,128)} %get-tuple-element.5.q_h, f32[512,1280]{1,0:T(8,128)} %get-tuple-element.6.k_h, f32[512,256]{1,0:T(8,128)} %get-tuple-element.7.inv, f32[1280]{0:T(1024)} %qg.1, f32[1280]{0:T(1024)} %kg.1), custom_call_target="tpu_custom_call" | custom-call | tf_op jit(solution)/shard_map/pallas_call | solution.py:417

commit v4 on v3

--- a/solution.py
+++ b/solution.py
@@ -281,7 +281,7 @@
             if i:
                 pl.when(n < 2)(lambda: out_copy(0, count_n - 2 + n, heads[0][3]).wait())
             v = dot(mod[...], w[:, at]) + bias[at].reshape(1, tile)
-            tiles[lax.rem(i * count_n + n, 2)] = v
+            tiles[lax.rem(i * count_n + n, 2)] = v.astype(BF16)
             sq[:, lanes] += lanes_sum(v * v)
             out_copy(i, n, dst).start()
             return carry
@@ -366,14 +366,14 @@
         V((count, half, span), BF16),
         V((cols, width), F32),
         V((tokens, width), BF16),
-        V((2, tokens, tile), F32),
+        V((2, tokens, tile), BF16),
         V((tokens, 256), F32),
         V((8, tokens), F32),
         V((count_t - 1, 8, tokens), F32),
     ]
     dma = pltpu.SemaphoreType.DMA
     scratch += [dma((12,)), dma((5,)), dma((5,)), dma((5,)), dma((count,)), dma((count,)), dma((count_t - 1,)), dma((count_t - 1,)), dma((2, part // 128))]
-    out = jax.ShapeDtypeStruct((tokens, part), F32)
+    out = jax.ShapeDtypeStruct((tokens, part), BF16)
     query, key, inv = pl.pallas_call(
         functools.partial(kernel, count_t, count_r),
         out_shape=(out, out, jax.ShapeDtypeStruct((tokens, 256), F32)),
@@ -403,7 +403,7 @@
             factor = inv[pl.ds(c * rows, rows), pl.ds(i * 128, 128)]
             for n in range(0, part, 128):
                 at = pl.ds(n, 128)
-                obuf[c, :, at] = (buf[c, :, at] * factor * gain[at].reshape(1, 128)).astype(BF16)
+                obuf[c, :, at] = (buf[c, :, at].astype(F32) * factor * gain[at].reshape(1, 128)).astype(BF16)
             stores[2 * c + i].start()
     for copy in stores:
         copy.wait()
@@ -420,7 +420,7 @@
         in_specs=[pl.BlockSpec(memory_space=pl.ANY)] * 2 + [pl.BlockSpec(memory_space=V)] * 3,
         out_specs=(pl.BlockSpec(memory_space=pl.ANY),) * 2,
         scratch_shapes=[
-            V((chunks, 128, part), F32), V((chunks, 128, part), F32), V((chunks, 128, part), BF16), V((chunks, 128, part), BF16),
+            V((chunks, 128, part), BF16), V((chunks, 128, part), BF16), V((chunks, 128, part), BF16), V((chunks, 128, part), BF16),
             dma((2, chunks)), dma((2, chunks)),
         ],
         compiler_params=pltpu.CompilerParams(vmem_limit_bytes=67043328),

time: 56.7 us -> 55.4 us (0.977)
  Pallas kernels: 55.9 us -> 54.6 us
    pallas_call x1, Pallas kernels: 5.05 us -> 3.74 us  [finish(): pl.pallas_call(scaled, out_shape=(out, out), in_specs=[pl.BlockSpec(memor...]
where the time goes in v4:
time: 55.4 us; the launch traced here: 55.2 us
  Pallas kernels  54.6 us (99%)
  between operations  0.64 us (1%)
    pallas_call x1, Pallas kernels, per_device(): pl.pallas_call(functools.partial(kernel, count_t, count_r), out_shape=(ou...  50.8 us
    pallas_call x1, Pallas kernels, finish(): pl.pallas_call(scaled, out_shape=(out, out), in_specs=[pl.BlockSpec(memor...  3.74 us

profile of v4, /device:TPU:0, one launch (start us, length us, event | category | flops | bytes accessed | tf_op | source)
XLA Modules:
  0.0 55.2 jit_solution(15542600945074490180)
XLA Ops:
  0.6 50.8 %shard_map.176 = (bf16[512,1280]{1,0:T(8,128)(2,1)}, bf16[512,1280]{1,0:T(8,128)(2,1)}, f32[512,256]{1,0:T(8,128)}) custom-call(s32[32]{0:T(128)} %packing.1, bf16[2,2,128,384]{3,2,1,0:T(8,128)(2,1)} %feat_h.1, f32[384]{0:T(512)} %gain_h.1, bf16[3,3,3,384,384]{4,3,2,1,0:T(8,128)(2,1)} %conv_h.1, f32[384]{0:T(512)} %cbias_h.1, bf16[16,384]{1,0:T(8,128)(2,1)} %bitcast.1, ...), custom_call_target="tpu_custom_call" | custom-call | tf_op jit(solution)/shard_map/pallas_call | solution.py:377
  51.5 3.7 %shard_map.177 = (bf16[512,1280]{1,0:T(8,128)(2,1)}, bf16[512,1280]{1,0:T(8,128)(2,1)}) custom-call(bf16[512,1280]{1,0:T(8,128)(2,1)} %get-tuple-element.5.q_h, bf16[512,1280]{1,0:T(8,128)(2,1)} %get-tuple-element.6.k_h, f32[512,256]{1,0:T(8,128)} %get-tuple-element.7.inv, f32[1280]{0:T(1024)} %qg.1, f32[1280]{0:T(1024)} %kg.1), custom_call_target="tpu_custom_call" | custom-call | tf_op jit(solution)/shard_map/pallas_call | solution.py:417
